TPU v7x, 32 devices: a whole 2x2x4 slice. The times are simulated.
32 devices in a mesh: wall: 16 (over z, y, x), stream: 2 (over core).
Axes of the slice: x: 2, y: 2, z: 4, core: 2. Of those that a mesh axis runs over, the one named last changes fastest.
Arguments:
- fields: float32 [5, 2, 3072, 2048], P(None, None, 'wall', 'stream'), may hold values from -5 to 5
- wall_velocity: float32 [2, 3072, 2048], P(None, 'wall', 'stream'), may hold values from -6 to 6
- diffusion: float32 [5], replicated, may hold values from 0.5 to 16
Outputs:
- tendency: float32 [5, 2, 3072, 2048], P(None, None, 'wall', 'stream')
- advanced: float32 [5, 2, 3072, 2048], P(None, None, 'wall', 'stream')
All inputs are finite; a program needn't handle non-finite values.
Results may differ from a plain program's by a relative error of at most 0.000094.
Values sent between devices are 32-bit elements; how exact they have to be, the bound alone decides.
A program may use at most 128 MiB of HBM per device.

v0:
```python
import jax
import jax.numpy as jnp
from jax import lax
from jax.sharding import PartitionSpec as P

compact_alpha = 1.0 / 3.0
compact_near = 14.0 / 9.0
compact_far = 1.0 / 9.0
time_step = 0.25
highest = lax.Precision.HIGHEST


def shifted_2(x, axis, by):
    count = lax.axis_size(axis)
    return lax.ppermute(x, axis, [(i, (i + by) % count) for i in range(count)])


def with_halo(cells, sides, width):
    for axis, dim in sides:
        count = lax.axis_size(axis)
        ends = count - 1
        head = lax.slice_in_dim(cells, 0, width, axis=dim)
        tail = lax.slice_in_dim(cells, cells.shape[dim] - width, cells.shape[dim], axis=dim)
        cells = jnp.concatenate(
            [
                lax.ppermute(tail, axis, [(i, (i + 1) % count) for i in range(ends)]),
                cells,
                lax.ppermute(head, axis, [((i + 1) % count, i) for i in range(ends)]),
            ],
            axis=dim,
        )
    return cells


def signed_power(base, exponent):
    safe_exponent = jnp.maximum(exponent, 0)
    magnitude = jnp.exp(safe_exponent.astype(jnp.float32) * jnp.log(jnp.abs(base)))
    odd_negative = jnp.logical_and(safe_exponent % 2 == 1, base < 0)
    return jnp.where(odd_negative, -magnitude, magnitude)


def band_roots(band, centre):
    spread = jnp.sqrt(centre * centre - 4.0 * band * band)
    larger = 0.5 * (centre + spread)
    ratio = 0.5 * (centre - spread) / larger
    return (larger, jnp.log(ratio), -band / larger)


def rising(log_ratio, exponent):
    return 1.0 - jnp.exp(jnp.asarray(exponent).astype(jnp.float32) * log_ratio)


def line_tables(band, centre, start, height):
    larger, log_ratio, base = band_roots(band, centre)
    larger3 = larger[:, None, None]
    ratio3 = log_ratio[:, None, None]
    base3 = base[:, None, None]
    ratio2 = log_ratio[:, None]
    base2 = base[:, None]
    rows = start + jnp.arange(height, dtype=jnp.int32)
    row_index = rows[:, None]
    col_index = rows[None, :]
    forward = jnp.where(
        row_index >= col_index,
        signed_power(base3, row_index - col_index)
        / larger3
        * rising(ratio3, col_index + 1)
        / rising(ratio3, row_index + 2),
        0.0,
    )
    backward = jnp.where(
        col_index >= row_index,
        signed_power(base3, col_index - row_index)
        * rising(ratio3, row_index + 1)
        / rising(ratio3, col_index + 1),
        0.0,
    )
    column = rows[None, :]
    entry = (
        signed_power(base2, column - start + 1)
        * rising(ratio2, start + 1)
        / rising(ratio2, column + 2)
    )
    ending = start + height
    leaving = (
        signed_power(base2, ending - column)
        * rising(ratio2, column + 1)
        / rising(ratio2, ending + 1)
    )
    return (forward, entry, backward, leaving)


def edge_tables(band, centre, start, height):
    larger, log_ratio, base = band_roots(band, centre)
    ratio2 = log_ratio[:, None]
    base2 = base[:, None]
    column = start + jnp.arange(height, dtype=jnp.int32)[None, :]
    entry = (
        signed_power(base2, column - start + 1)
        * rising(ratio2, start + 1)
        / rising(ratio2, column + 2)
    )
    first_row = (
        signed_power(base2, column - start) * rising(ratio2, start + 1) / rising(ratio2, column + 1)
    )
    leave_first = (
        signed_power(base2, jnp.full((1, 1), height, jnp.int32))
        * rising(ratio2, start + 1)
        / rising(ratio2, start + height + 1)
    )[:, 0]
    through = jnp.sum(first_row * entry, axis=1)
    return (entry[:, -1], leave_first, through)


def line_solve(source, band, centre):
    height = source.shape[2]
    start = lax.axis_index("wall") * height
    forward, entry, backward, leaving = line_tables(band, centre, start, height)
    local = jnp.einsum("fji,fzix->fzjx", forward, source, precision=highest)
    heading = jnp.einsum("fl,fzlx->fzx", backward[:, 0, :], local, precision=highest)
    tails, heads = (
        lax.all_gather(local[None, :, :, -1, :], "wall", axis=0, tiled=True),
        lax.all_gather(heading[None], "wall", axis=0, tiled=True),
    )
    count = lax.axis_size("wall")
    member = lax.axis_index("wall")
    tables = [edge_tables(band, centre, device * height, height) for device in range(count)]
    current = jnp.zeros_like(heading)
    incoming = []
    arriving = jnp.zeros_like(heading)
    for device in range(count):
        incoming.append(current)
        arriving = jnp.where(member == device, current, arriving)
        current = tables[device][0][:, None, None] * current + tails[device]
    outgoing = jnp.zeros_like(heading)
    beyond = jnp.zeros_like(heading)
    for device in reversed(range(count)):
        beyond = jnp.where(member == device, outgoing, beyond)
        outgoing = (
            tables[device][1][:, None, None] * outgoing
            + tables[device][2][:, None, None] * incoming[device]
            + heads[device]
        )
    primed = local + entry[:, None, :, None] * arriving[:, :, None, :]
    settled = jnp.einsum("fjl,fzlx->fzjx", backward, primed, precision=highest)
    return settled + leaving[:, None, :, None] * beyond[:, :, None, :]


def on_device(fields, wall_velocity, diffusion):
    count_fields = fields.shape[0]
    width = fields.shape[3]
    height = fields.shape[2]
    first_cols = jnp.swapaxes(fields[:, :, :, :3], 2, 3)
    last_cols = jnp.swapaxes(fields[:, :, :, width - 3 :], 2, 3)
    below = shifted_2(last_cols, "stream", 1)
    above = shifted_2(first_cols, "stream", -1)
    padded = jnp.concatenate([jnp.swapaxes(below, 2, 3), fields, jnp.swapaxes(above, 2, 3)], axis=3)

    def shifted(offset):
        return padded[:, :, :, 3 + offset : 3 + offset + width]

    streamwise = (
        45.0 * (shifted(1) - shifted(-1))
        - 9.0 * (shifted(2) - shifted(-2))
        + (shifted(3) - shifted(-3))
    ) / 60.0
    rimmed = with_halo(fields, (("wall", 2),), 2)

    def layer(offset):
        return rimmed[:, :, 2 + offset : 2 + offset + height, :]

    source = 0.5 * compact_near * (layer(1) - layer(-1)) + 0.25 * compact_far * (
        layer(2) - layer(-2)
    )
    unit_bands = jnp.ones((count_fields,), jnp.float32)
    normal_slope = line_solve(source, compact_alpha * unit_bands, unit_bands)
    tendency = -(fields[0][None] * streamwise + wall_velocity[None] * normal_slope)
    smoothed = line_solve(2.0 * fields + time_step * tendency, -diffusion, 1.0 + 2.0 * diffusion)
    return (tendency, smoothed - fields)


def solution(mesh):
    in_specs = (P(None, None, "wall", "stream"), P(None, "wall", "stream"), P())
    out_specs = (P(None, None, "wall", "stream"), P(None, None, "wall", "stream"))
    return jax.shard_map(
        on_device, mesh=mesh, in_specs=in_specs, out_specs=out_specs, check_vma=False
    )
```

profile of v0, /device:TPU:0, one launch (start us, length us, event | category | flops | bytes accessed | tf_op | source)
XLA Modules:
  0.0 335.9 jit_solution(16098397129262669655)
XLA Ops:
  0.6 1.8 fusion.199
  2.4 1.3 collective-permute-start.2
  3.7 6.1 %collective-permute-start.3 = (f32[5,2,2,1024]{3,2,1,0:T(2,128)}, f32[5,2,2,1024]{3,2,1,0:T(2,128)}, u32[]{:S(2)}, u32[]{:S(2)}) collective-permute-start(f32[5,2,2,1024]{3,2,1,0:T(2,128)} %get-tuple-element.38), channel_id=1, source_target_pairs={{0,2},{2,4},{4,6},{6,8},{8,10},{10,12},{12,14},{14,16},{16,18},{18... | collective-permute-start | bytes 245768 | tf_op jit(solution)/shard_map/ppermute | solution.py:26
  9.9 1.8 fusion.200
  11.7 1.0 copy.148
  15.5 1.3 multiply_divide_fusion.15
  17.4 0.9 broadcast_compare_fusion
  18.4 0.9 fusion.103
  19.3 1.7 multiply_bitcast_fusion
  21.1 7.8 %constant_dynamic-update-slice_fusion.1 = f32[5,2,194,1024]{3,2,1,0:T(8,128)} fusion(f32[5,2,192,1024]{3,2,1,0:T(8,128)} %param.3), kind=kLoop, calls=%fused_computation.317 | loop fusion | bytes 15728640
  30.2 0.8 multiply_reduce_fusion.14
  31.0 0.8 slice_reduce_fusion.3
  31.8 0.8 slice_reduce_fusion.1
  32.6 0.8 slice_reduce_fusion.2
  33.3 0.8 multiply_reduce_fusion.13
  34.8 0.7 slice_reduce_fusion.4
  36.3 0.8 slice_reduce_fusion.5
  37.1 0.8 multiply_reduce_fusion.12
  40.0 0.8 slice_reduce_fusion.8
  40.7 1.3 fusion.167
  42.0 0.8 slice_reduce_fusion.26
  42.8 0.8 slice_reduce_fusion.14
  43.5 0.8 slice_reduce_fusion.25
  44.3 1.4 multiply_reduce_fusion.11
  45.7 0.8 slice_reduce_fusion.11
  47.8 0.8 fusion.151
  48.6 0.8 slice_reduce_fusion.19
  51.5 0.7 slice_reduce_fusion.16
  55.8 0.8 slice_reduce_fusion.22
  56.6 1.4 fusion.175
  57.9 1.3 fusion.176
  59.9 1.8 fusion.61
  62.3 1.3 copy.105
  63.7 1.3 copy.107
  65.0 1.6 constant_dynamic-update-slice_fusion
  66.6 17.3 %fusion.49 = f32[5,2,192,1024]{3,2,1,0:T(8,128)S(1)} fusion(f32[5,2,2,1024]{3,2,1,0:T(2,128)} %collective-permute-done.3, f32[5,2,192,1024]{3,2,1,0:T(8,128)} %param.3, f32[5,2,194,1024]{3,2,1,0:T(8,128)} %constant_dynamic-update-slice_fusion, f32[192]{0:T(256)} %copy-done.44, f32[192]{0:T(256)} %get-tuple-element.124, f32[192,192]{1,0:T(8,128)} %get-tuple-element.99, ...), kind=kOutput, calls=%fused_computation.60 | convolution fusion | flops 4544348160 | bytes 32032768 | tf_op jit(solution)/shard_map/fji,fzix->fzjx/dot_general | solution.py:119
  84.3 2.9 copy-done
  87.2 4.6 %fusion.170 = f32[5,1,2,1024]{3,1,2,0:T(1,128)S(1)} fusion(f32[5,2,192,1024]{3,2,1,0:T(8,128)S(1)} %fusion.49, f32[5,192,192]{2,1,0:T(8,128)} %get-tuple-element.42), kind=kOutput, calls=%fused_computation.321 | convolution fusion | flops 23592960 | bytes 7910400 | tf_op jit(solution)/shard_map/fl,fzlx->fzx/dot_general | solution.py:120
  91.8 43.1 %all-gather = f32[80,2,1,1024]{3,1,2,0:T(2,128)S(1)} all-gather(f32[5,2,1,1024]{3,1,2,0:T(2,128)S(1)} %copy.108), channel_id=2, replica_groups=mesh['wall'=16,'stream'=2] {'wall'}, dimensions={0}, use_global_device_ids=true | all-gather | bytes 696320 | tf_op jit(solution)/shard_map/all_gather | solution.py:122
  134.9 39.4 %all-gather.1 = f32[80,2,1024]{2,1,0:T(2,128)S(1)} all-gather(f32[5,2,1024]{2,1,0:T(2,128)S(1)} %bitcast.331), channel_id=3, replica_groups=mesh['wall'=16,'stream'=2] {'wall'}, dimensions={0}, use_global_device_ids=true | all-gather | bytes 696320 | tf_op jit(solution)/shard_map/all_gather | solution.py:123
  174.9 0.8 fusion.120
  175.8 44.5 %fusion.13 = f32[5,2,192,1024]{3,2,1,0:T(8,128)} fusion(f32[5,2,192,1024]{3,2,1,0:T(8,128)} %param.3, f32[5,2,192,3]{3,2,1,0:T(8,128)} %bitcast.330, f32[5,2,192,3]{3,2,1,0:T(8,128)} %bitcast.329, f32[5,2,1024]{2,1,0:T(2,128)S(1)} %fusion.120, f32[5,192]{1,0:T(8,128)} %get-tuple-element.102, f32[2,192,1024]{2,1,0:T(8,128)} %param.4, ...), kind=kOutput, calls=%fused_computation.22 | convolution fusion | flops 4571873280 | bytes 29284352 | tf_op jit(solution)/shard_map/fjl,fzlx->fzjx/dot_general | solution.py:145
  220.4 13.1 %fusion.46 = f32[5,2,192,1024]{3,2,1,0:T(8,128)S(1)} fusion(f32[5,2,192,1024]{3,2,1,0:T(8,128)} %fusion.13, f32[5,2,192,1024]{3,2,1,0:T(8,128)} %param.3, f32[5,192]{1,0:T(8,128)S(1)} %copy-done.7, f32[5,192]{1,0:T(8,128)S(1)} %get-tuple-element.77, f32[5]{0:T(128)S(1)} %copy-done.12, f32[5]{0:T(128)S(1)} %get-tuple-element.105, ...), kind=kOutput, calls=%fused_computation.59 | convolution fusion | flops 4537221120 | bytes 23821868 | tf_op jit(solution)/shard_map/fji,fzix->fzjx/dot_general | solution.py:119
  233.9 4.6 %fusion.169 = f32[5,1,2,1024]{3,1,2,0:T(1,128)S(1)} fusion(f32[5,2,192,1024]{3,2,1,0:T(8,128)S(1)} %fusion.46, f32[5,192,192]{2,1,0:T(8,128)} %get-tuple-element.41), kind=kOutput, calls=%fused_computation.319 | convolution fusion | flops 23592960 | bytes 7910400 | tf_op jit(solution)/shard_map/fl,fzlx->fzx/dot_general | solution.py:120
  238.6 41.9 %all-gather.2 = f32[80,2,1,1024]{3,1,2,0:T(2,128)S(1)} all-gather(f32[5,2,1,1024]{3,1,2,0:T(2,128)S(1)} %copy.123), channel_id=4, replica_groups=mesh['wall'=16,'stream'=2] {'wall'}, dimensions={0}, use_global_device_ids=true | all-gather | bytes 696320 | tf_op jit(solution)/shard_map/all_gather | solution.py:122
  280.4 40.0 %all-gather.3 = f32[80,2,1024]{2,1,0:T(2,128)S(1)} all-gather(f32[5,2,1024]{2,1,0:T(2,128)S(1)} %bitcast.332), channel_id=5, replica_groups=mesh['wall'=16,'stream'=2] {'wall'}, dimensions={0}, use_global_device_ids=true | all-gather | bytes 696320 | tf_op jit(solution)/shard_map/all_gather | solution.py:123
  321.2 1.5 fusion.104
  322.7 12.7 %fusion.26 = f32[5,2,192,1024]{3,2,1,0:T(8,128)} fusion(f32[5,2,192,1024]{3,2,1,0:T(8,128)S(1)} %bitcast.324, f32[5,2,1024]{2,1,0:T(2,128)S(1)} %fusion.104, f32[5,192]{1,0:T(8,128)S(1)} %copy-done.8, f32[5,2,192,1024]{3,2,1,0:T(8,128)S(1)} %fusion.46, f32[5,2,1024]{2,1,0:T(2,128)S(1)} %select_select_fusion, f32[5,192]{1,0:T(8,128)S(1)} %get-tuple-element.71, ...), kind=kOutput, calls=%fused_computation.38 | convolution fusion | flops 4540968960 | bytes 23907608 | tf_op jit(solution)/shard_map/fjl,fzlx->fzjx/dot_general | solution.py:145
  (244 shorter events, 17.6 us)
Async XLA Ops:
  2.4 62.6 %collective-permute-start.2 = (f32[5,2,2,1024]{3,2,1,0:T(2,128)}, f32[5,2,2,1024]{3,2,1,0:T(2,128)}, u32[]{:S(2)}, u32[]{:S(2)}) collective-permute-start(f32[5,2,2,1024]{3,2,1,0:T(2,128)} %get-tuple-element.37), channel_id=1, source_target_pairs={{2,0},{4,2},{6,4},{8,6},{10,8},{12,10},{14,12},{16,14},{18,16},{20... | collective-permute-start | bytes 245768 | tf_op jit(solution)/shard_map/ppermute | solution.py:28
  3.7 62.9 %collective-permute-start.3 = (f32[5,2,2,1024]{3,2,1,0:T(2,128)}, f32[5,2,2,1024]{3,2,1,0:T(2,128)}, u32[]{:S(2)}, u32[]{:S(2)}) collective-permute-start(f32[5,2,2,1024]{3,2,1,0:T(2,128)} %get-tuple-element.38), channel_id=1, source_target_pairs={{0,2},{2,4},{4,6},{6,8},{8,10},{10,12},{12,14},{14,16},{16,18},{18... | collective-permute-start | bytes 245768 | tf_op jit(solution)/shard_map/ppermute | solution.py:26
  12.7 50.9 %collective-permute-start.1 = (f32[5,2,3,192]{3,1,2,0:T(2,128)}, f32[5,2,3,192]{3,1,2,0:T(2,128)S(1)}, u32[]{:S(2)}, u32[]{:S(2)}) collective-permute-start(f32[5,2,3,192]{3,1,2,0:T(2,128)} %bitcast.2), channel_id=1, source_target_pairs={{0,1},{1,0},{2,3},{3,2},{4,5},{5,4},{6,7},{7,6},{8,9},{9,8},{10,11... | collective-permute-start | bytes 69128 | tf_op jit(solution)/shard_map/ppermute | solution.py:15
  13.1 49.2 %collective-permute-start = (f32[5,2,3,192]{3,1,2,0:T(2,128)S(1)}, f32[5,2,3,192]{3,1,2,0:T(2,128)S(1)}, u32[]{:S(2)}, u32[]{:S(2)}) collective-permute-start(f32[5,2,3,192]{3,1,2,0:T(2,128)S(1)} %bitcast.333), channel_id=1, source_target_pairs={{0,1},{1,0},{2,3},{3,2},{4,5},{5,4},{6,7},{7,6},{8,9},{9,8},{10,11... | collective-permute-start | bytes 69128 | tf_op jit(solution)/shard_map/ppermute | solution.py:15
  84.0 90.3 %copy-start.29 = (f32[5]{0:T(128)S(1)}, f32[5]{0:T(128)}, u32[]{:S(2)}) copy-start(f32[5]{0:T(128)} %slice_reduce_fusion.26) | copy-start | bytes 64
  84.0 90.3 %copy-start.30 = (f32[5]{0:T(128)S(1)}, f32[5]{0:T(128)}, u32[]{:S(2)}) copy-start(f32[5]{0:T(128)} %slice_reduce_fusion.14) | copy-start | bytes 64
  84.0 90.3 %copy-start.31 = (f32[5]{0:T(128)S(1)}, f32[5]{0:T(128)}, u32[]{:S(2)}) copy-start(f32[5]{0:T(128)} %slice_reduce_fusion.25) | copy-start | bytes 64
  84.0 90.3 %copy-start.32 = (f32[5]{0:T(128)S(1)}, f32[5]{0:T(128)}, u32[]{:S(2)}) copy-start(f32[5]{0:T(128)} %slice_reduce_fusion.19) | copy-start | bytes 64
  84.0 90.3 %copy-start.33 = (f32[5]{0:T(128)S(1)}, f32[5]{0:T(128)}, u32[]{:S(2)}) copy-start(f32[5]{0:T(128)} %slice_reduce_fusion.15) | copy-start | bytes 64
  84.0 90.3 %copy-start.34 = (f32[5]{0:T(128)S(1)}, f32[5]{0:T(128)}, u32[]{:S(2)}) copy-start(f32[5]{0:T(128)} %slice_reduce_fusion.18) | copy-start | bytes 64
  84.0 90.3 %copy-start.35 = (f32[5]{0:T(128)S(1)}, f32[5]{0:T(128)}, u32[]{:S(2)}) copy-start(f32[5]{0:T(128)} %slice_reduce_fusion.17) | copy-start | bytes 64
  84.0 90.3 %copy-start.36 = (f32[5]{0:T(128)S(1)}, f32[5]{0:T(128)}, u32[]{:S(2)}) copy-start(f32[5]{0:T(128)} %slice_reduce_fusion.16) | copy-start | bytes 64
  84.0 90.3 %copy-start.37 = (f32[5]{0:T(128)S(1)}, f32[5]{0:T(128)}, u32[]{:S(2)}) copy-start(f32[5]{0:T(128)} %slice_reduce_fusion.27) | copy-start | bytes 64
  84.1 90.3 %copy-start.38 = (f32[5]{0:T(128)S(1)}, f32[5]{0:T(128)}, u32[]{:S(2)}) copy-start(f32[5]{0:T(128)} %slice_reduce_fusion.20) | copy-start | bytes 64
  84.1 90.3 %copy-start.39 = (f32[5]{0:T(128)S(1)}, f32[5]{0:T(128)}, u32[]{:S(2)}) copy-start(f32[5]{0:T(128)} %slice_reduce_fusion.24) | copy-start | bytes 64
  84.1 90.3 %copy-start.40 = (f32[5]{0:T(128)S(1)}, f32[5]{0:T(128)}, u32[]{:S(2)}) copy-start(f32[5]{0:T(128)} %slice_reduce_fusion.23) | copy-start | bytes 64
  84.1 90.3 %copy-start.41 = (f32[5]{0:T(128)S(1)}, f32[5]{0:T(128)}, u32[]{:S(2)}) copy-start(f32[5]{0:T(128)} %slice_reduce_fusion.22) | copy-start | bytes 64
  84.1 90.3 %copy-start.42 = (f32[5]{0:T(128)S(1)}, f32[5]{0:T(128)}, u32[]{:S(2)}) copy-start(f32[5]{0:T(128)} %fusion.175) | copy-start | bytes 64
  84.1 90.3 %copy-start.43 = (f32[5]{0:T(128)S(1)}, f32[5]{0:T(128)}, u32[]{:S(2)}) copy-start(f32[5]{0:T(128)} %slice_reduce_fusion.21) | copy-start | bytes 64
  84.1 90.7 %copy-start.65 = (f32[5]{0:T(128)S(1)}, f32[5]{0:T(128)}, u32[]{:S(2)}) copy-start(f32[5]{0:T(128)} %get-tuple-element.14) | copy-start | bytes 64
  84.1 90.7 %copy-start.66 = (f32[5]{0:T(128)S(1)}, f32[5]{0:T(128)}, u32[]{:S(2)}) copy-start(f32[5]{0:T(128)} %get-tuple-element.15) | copy-start | bytes 64
  84.1 90.7 %copy-start.67 = (f32[5]{0:T(128)S(1)}, f32[5]{0:T(128)}, u32[]{:S(2)}) copy-start(f32[5]{0:T(128)} %get-tuple-element.16) | copy-start | bytes 64
  84.1 90.7 %copy-start.68 = (f32[5]{0:T(128)S(1)}, f32[5]{0:T(128)}, u32[]{:S(2)}) copy-start(f32[5]{0:T(128)} %get-tuple-element.2) | copy-start | bytes 64
  84.2 90.7 %copy-start.69 = (f32[5]{0:T(128)S(1)}, f32[5]{0:T(128)}, u32[]{:S(2)}) copy-start(f32[5]{0:T(128)} %get-tuple-element.3) | copy-start | bytes 64
  84.2 90.7 %copy-start.70 = (f32[5]{0:T(128)S(1)}, f32[5]{0:T(128)}, u32[]{:S(2)}) copy-start(f32[5]{0:T(128)} %get-tuple-element.4) | copy-start | bytes 64
  84.2 90.7 %copy-start.71 = (f32[5]{0:T(128)S(1)}, f32[5]{0:T(128)}, u32[]{:S(2)}) copy-start(f32[5]{0:T(128)} %get-tuple-element.5) | copy-start | bytes 64
  84.2 90.7 %copy-start.72 = (f32[5]{0:T(128)S(1)}, f32[5]{0:T(128)}, u32[]{:S(2)}) copy-start(f32[5]{0:T(128)} %get-tuple-element.6) | copy-start | bytes 64
  84.2 90.7 %copy-start.73 = (f32[5]{0:T(128)S(1)}, f32[5]{0:T(128)}, u32[]{:S(2)}) copy-start(f32[5]{0:T(128)} %get-tuple-element.7) | copy-start | bytes 64
  84.2 90.7 %copy-start.74 = (f32[5]{0:T(128)S(1)}, f32[5]{0:T(128)}, u32[]{:S(2)}) copy-start(f32[5]{0:T(128)} %get-tuple-element.8) | copy-start | bytes 64
  84.2 90.7 %copy-start.75 = (f32[5]{0:T(128)S(1)}, f32[5]{0:T(128)}, u32[]{:S(2)}) copy-start(f32[5]{0:T(128)} %get-tuple-element.9) | copy-start | bytes 64
  84.2 90.7 %copy-start.76 = (f32[5]{0:T(128)S(1)}, f32[5]{0:T(128)}, u32[]{:S(2)}) copy-start(f32[5]{0:T(128)} %get-tuple-element.10) | copy-start | bytes 64
  84.2 90.7 %copy-start.77 = (f32[5]{0:T(128)S(1)}, f32[5]{0:T(128)}, u32[]{:S(2)}) copy-start(f32[5]{0:T(128)} %get-tuple-element.11) | copy-start | bytes 64
  84.2 90.7 %copy-start.78 = (f32[5]{0:T(128)S(1)}, f32[5]{0:T(128)}, u32[]{:S(2)}) copy-start(f32[5]{0:T(128)} %get-tuple-element.12) | copy-start | bytes 64
  84.3 90.7 %copy-start.79 = (f32[5]{0:T(128)S(1)}, f32[5]{0:T(128)}, u32[]{:S(2)}) copy-start(f32[5]{0:T(128)} %get-tuple-element.13) | copy-start | bytes 64
  220.3 102.3 %slice-start = ((s8[7864320]{0:T(1024)(128)(4,1)}), s8[4194304]{0:T(1024)(128)(4,1)S(1)}, s32[]{:S(2)}) async-start(s8[7864320]{0:T(1024)(128)(4,1)} %bitcast.323), calls=%async_computation | async-start | bytes 8388608
  220.4 102.3 %slice-start.1 = ((s8[7864320]{0:T(1024)(128)(4,1)}), s8[3670016]{0:T(1024)(128)(4,1)S(1)}, s32[]{:S(2)}) async-start(s8[7864320]{0:T(1024)(128)(4,1)} %bitcast.323), calls=%async_computation.1 | async-start | bytes 7340032
  233.7 87.3 %copy-start.45 = (f32[5]{0:T(128)S(1)}, f32[5]{0:T(128)}, u32[]{:S(2)}) copy-start(f32[5]{0:T(128)} %get-tuple-element.17) | copy-start | bytes 64
  233.7 87.3 %copy-start.46 = (f32[5]{0:T(128)S(1)}, f32[5]{0:T(128)}, u32[]{:S(2)}) copy-start(f32[5]{0:T(128)} %get-tuple-element.18) | copy-start | bytes 64
  233.7 87.3 %copy-start.47 = (f32[5]{0:T(128)S(1)}, f32[5]{0:T(128)}, u32[]{:S(2)}) copy-start(f32[5]{0:T(128)} %get-tuple-element.19) | copy-start | bytes 64
  233.7 87.3 %copy-start.48 = (f32[5]{0:T(128)S(1)}, f32[5]{0:T(128)}, u32[]{:S(2)}) copy-start(f32[5]{0:T(128)} %get-tuple-element.20) | copy-start | bytes 64
  233.7 87.3 %copy-start.49 = (f32[5]{0:T(128)S(1)}, f32[5]{0:T(128)}, u32[]{:S(2)}) copy-start(f32[5]{0:T(128)} %get-tuple-element.21) | copy-start | bytes 64
  233.7 87.3 %copy-start.50 = (f32[5]{0:T(128)S(1)}, f32[5]{0:T(128)}, u32[]{:S(2)}) copy-start(f32[5]{0:T(128)} %get-tuple-element.22) | copy-start | bytes 64
  233.7 87.3 %copy-start.51 = (f32[5]{0:T(128)S(1)}, f32[5]{0:T(128)}, u32[]{:S(2)}) copy-start(f32[5]{0:T(128)} %get-tuple-element.23) | copy-start | bytes 64
  233.7 87.3 %copy-start.52 = (f32[5]{0:T(128)S(1)}, f32[5]{0:T(128)}, u32[]{:S(2)}) copy-start(f32[5]{0:T(128)} %get-tuple-element.24) | copy-start | bytes 64
  233.7 87.3 %copy-start.53 = (f32[5]{0:T(128)S(1)}, f32[5]{0:T(128)}, u32[]{:S(2)}) copy-start(f32[5]{0:T(128)} %get-tuple-element.25) | copy-start | bytes 64
  233.8 87.3 %copy-start.54 = (f32[5]{0:T(128)S(1)}, f32[5]{0:T(128)}, u32[]{:S(2)}) copy-start(f32[5]{0:T(128)} %get-tuple-element.26) | copy-start | bytes 64
  233.8 88.9 %copy-start.2 = (pred[192,192]{1,0:T(8,128)(4,1)S(1)}, pred[192,192]{1,0:T(8,128)(4,1)}, u32[]{:S(2)}) copy-start(pred[192,192]{1,0:T(8,128)(4,1)} %copy-done.1) | copy-start | bytes 110596
  233.8 88.9 %copy-start.8 = (f32[5,192]{1,0:T(8,128)S(1)}, f32[5,192]{1,0:T(8,128)}, u32[]{:S(2)}) copy-start(f32[5,192]{1,0:T(8,128)} %get-tuple-element.76) | copy-start | bytes 11524
  (38 other events, 2654.9 us)
where the time goes:
time: 341 us; the launch traced here: 336 us
  blocking collectives  164 us (48%)
  matrix products  96.8 us (28%)
  local copies, waits for them, and re-layouts  42.1 us (12%)
  other arithmetic  21.9 us (6%)
  starting transfers between devices  7.95 us (2%)
    all_gather x2, blocking collectives, line_solve(): lax.all_gather(local[None, :, :, -1, :], 'wall', axis=0, tiled=True)  85 us
    all_gather x2, blocking collectives, line_solve(): lax.all_gather(heading[None], 'wall', axis=0, tiled=True)  79.4 us
    dot_general x2, matrix products, line_solve(): settled = jnp.einsum('fjl,fzlx->fzjx', backward, primed, precision=highest)  57.2 us
    dot_general x2, matrix products, line_solve(): local = jnp.einsum('fji,fzix->fzjx', forward, source, precision=highest)  30.4 us
    slice x30, local copies, waits for them, and re-layouts, edge_tables(): return (entry[:, -1], leave_first, through)  21.6 us
    unnamed x167, local copies, waits for them, and re-layouts  12.4 us
    dot_general x2, matrix products, line_solve(): jnp.einsum('fl,fzlx->fzx', backward[:, 0, :], local, precision=highest)  9.13 us
  transfers between devices with their start and end apart: 4, of which 0 were waited for; matrix products, arithmetic and copies ran while one was open for 17% of the time, Pallas kernels for 0%

commit v1 on v0

v1 whole, which is shorter than its diff:
```python
import functools
import math

import jax
import jax.numpy as jnp
import numpy as np
from jax import lax
from jax.experimental import pallas as pl
from jax.experimental.pallas import tpu as pltpu
from jax.sharding import PartitionSpec as P

MESH = pl.DeviceIdType.MESH
compact_alpha = 1.0 / 3.0
compact_near = 14.0 / 9.0
compact_far = 1.0 / 9.0
time_step = 0.25
lane = 128
sub = 8


def compact_operator(height):
    band = compact_alpha
    a = np.eye(height) + band * (np.eye(height, k=1) + np.eye(height, k=-1))
    wide = np.zeros((height, height + 4))
    for j in range(height):
        wide[j, j + 3] += 0.5 * compact_near
        wide[j, j + 1] -= 0.5 * compact_near
        wide[j, j + 4] += 0.25 * compact_far
        wide[j, j] -= 0.25 * compact_far
    source = np.concatenate(
        [wide[:, 2 : height + 2], wide[:, :2], wide[:, height + 2 :], np.zeros((height, 2))], axis=1
    )
    source[0, height + 4] = -band
    source[height - 1, height + 5] = -band
    return np.linalg.solve(a, source)


def merge_table(gamma, eta, count, me):
    like = gamma + 0.0 * me.astype(jnp.float32)
    ll, lr, rl, rr = 1.0 + 0.0 * like, 0.0 * like, 0.0 * like, 1.0 + 0.0 * like
    rows = []
    bit = 1
    while bit < count:
        right = (me // bit) % 2 == 1
        inv = 1.0 / (1.0 - gamma * gamma)
        near, far = inv * eta, inv * eta * gamma
        add_l = jnp.where(right, ll, lr)
        add_r = jnp.where(right, rl, rr)
        rows.append(jnp.stack([inv, gamma, eta, add_l, add_r]))
        ll, lr = (
            jnp.where(right, ll * near, ll + lr * far),
            jnp.where(right, lr + ll * far, lr * near),
        )
        rl, rr = (
            jnp.where(right, rl * near, rl + rr * far),
            jnp.where(right, rr + rl * far, rr * near),
        )
        gamma, eta = gamma + eta * eta * gamma * inv, eta * eta * inv
        bit *= 2
    return jnp.stack(rows).reshape(-1)


def row_to_tile(dst, row):
    for t in range(row.shape[-1] // lane):
        dst[t : t + 1, :] = row[:, t * lane : (t + 1) * lane]


def partners(count):
    me = lax.axis_index("wall")
    out = []
    bit = 1
    while bit < count:
        out.append((bit, me + bit * (1 - 2 * ((me // bit) % 2))))
        bit *= 2
    return me, out


def exchange(count, nf, table, buf, got, send, recv, xl, xr):
    me, others = partners(count)
    per = buf.shape[2] // nf
    xl[...] = jnp.zeros(xl.shape, jnp.float32)
    xr[...] = jnp.zeros(xr.shape, jnp.float32)
    for s, (bit, other) in enumerate(others):
        copy = pltpu.make_async_remote_copy(
            src_ref=buf.at[s],
            dst_ref=got.at[s],
            send_sem=send.at[s],
            recv_sem=recv.at[s],
            device_id={"wall": other},
            device_id_type=MESH,
        )
        copy.start()
        copy.wait()
        right = (me // bit) % 2 == 1
        for k in range(nf):
            at = pl.ds(k * per, per)
            inv, gamma, eta, add_l, add_r = (table[(s * 5 + c) * nf + k] for c in range(5))
            fo, lo, fp, lp = buf[s, 0, at], buf[s, 1, at], got[s, 0, at], got[s, 1, at]
            f1, l1 = jnp.where(right, fp, fo), jnp.where(right, lp, lo)
            f2, l2 = jnp.where(right, fo, fp), jnp.where(right, lo, lp)
            head = inv * (f2 + gamma * l1)
            tail = inv * (l1 + gamma * f2)
            value = jnp.where(right, tail, head)
            xl[at] += add_l * value
            xr[at] += add_r * value
            if s + 1 < len(others):
                buf[s + 1, 0, at] = f1 + eta * head
                buf[s + 1, 1, at] = l2 + eta * tail


def first_kernel(count, streams, nf, ends, table, coef, fields, bc, strips, planes, edge, halo, sides,
                 got_strip, buf, got, xl, xr, local_sem, hs, hr, ss, sr, send, recv):
    me, others = partners(count)
    np_, height, width = planes.shape
    strip = sides.shape[2]
    tops = pltpu.make_async_copy(fields.at[:, pl.ds(0, sub)], edge.at[0], local_sem.at[np_])
    bots = pltpu.make_async_copy(fields.at[:, pl.ds(height - sub, sub)], edge.at[1], local_sem.at[np_ + 1])
    tops.start()
    bots.start()
    loads = [
        pltpu.make_async_copy(fields.at[p], planes.at[p], local_sem.at[p]) for p in range(np_)
    ]
    for load in loads:
        load.start()
    halo[2:4] = jnp.zeros((2,) + halo.shape[1:], jnp.float32)
    col = lax.axis_index("stream")
    nexts = [lax.rem(col + 1, streams)] if streams == 2 else [
        lax.rem(col + 1, streams), lax.rem(col + streams - 1, streams)]
    has_left, has_right = me > 0, me < count - 1
    barrier = pltpu.get_barrier_semaphore()
    for _, other in others:
        pl.semaphore_signal(barrier, inc=1, device_id={"wall": other}, device_id_type=MESH)
    for other in nexts:
        pl.semaphore_signal(barrier, inc=1, device_id={"stream": other}, device_id_type=MESH)

    @pl.when(has_left)
    def _():
        pl.semaphore_signal(barrier, inc=1, device_id={"wall": me - 1}, device_id_type=MESH)

    @pl.when(has_right)
    def _():
        pl.semaphore_signal(barrier, inc=1, device_id={"wall": me + 1}, device_id_type=MESH)

    tops.wait()
    bots.wait()
    for p in range(np_):
        for r in range(2):
            row_to_tile(halo.at[0, r, p], edge[0, p, r : r + 1, :])
            row_to_tile(halo.at[1, r, p], edge[1, p, sub - 2 + r : sub - 1 + r, :])
    pl.semaphore_wait(
        barrier,
        len(others) + len(nexts) + has_left.astype(jnp.int32) + has_right.astype(jnp.int32),
    )

    to_left = pltpu.make_async_remote_copy(
        src_ref=halo.at[0], dst_ref=halo.at[3], send_sem=hs.at[0], recv_sem=hr.at[0],
        device_id={"wall": me - 1}, device_id_type=MESH)
    to_right = pltpu.make_async_remote_copy(
        src_ref=halo.at[1], dst_ref=halo.at[2], send_sem=hs.at[1], recv_sem=hr.at[1],
        device_id={"wall": me + 1}, device_id_type=MESH)

    @pl.when(has_left)
    def _():
        to_left.start()

    @pl.when(has_right)
    def _():
        to_right.start()

    low = lax.broadcasted_iota(jnp.int32, (height, strip), 1) < strip // 2
    step = 256
    for p in range(np_):
        loads[p].wait()
        sides[p] = jnp.where(low, planes[p, :, :strip], planes[p, :, width - strip :])
        for c in range(0, width, step):
            f = planes[p, :, c : c + step]
            for e in range(2):
                w = coef[e]
                row = jnp.sum(f * jnp.concatenate([w] * (step // lane), axis=1), axis=0, keepdims=True)
                for t in range(step // lane):
                    buf[0, e, p, c // lane + t : c // lane + t + 1, :] = row[:, t * lane : (t + 1) * lane]
    side_copies = [
        pltpu.make_async_remote_copy(
            src_ref=sides, dst_ref=got_strip.at[i], send_sem=ss.at[i], recv_sem=sr.at[i],
            device_id={"stream": other}, device_id_type=MESH)
        for i, other in enumerate(nexts)
    ]
    for copy in side_copies:
        copy.start()

    @pl.when(has_left)
    def _():
        to_left.wait_send()
        to_right.wait_recv()

    @pl.when(has_right)
    def _():
        to_right.wait_send()
        to_left.wait_recv()

    for e in range(2):
        buf[0, e] = (buf[0, e] + ends[e][0] * halo[2, 0] + ends[e][1] * halo[2, 1]
                     + ends[e][2] * halo[3, 0] + ends[e][3] * halo[3, 1])
    exchange(count, nf, table, buf, got, send, recv, xl, xr)
    for r in range(2):
        bc[r] = halo[2, r]
        bc[2 + r] = halo[3, r]
    bc[4] = xl[...]
    bc[5] = xr[...]
    for copy in side_copies:
        copy.wait()
    strips[...] = got_strip[...]


def second_kernel(count, nf, table, q_edges, out, buf, got, xl, xr, send, recv):
    _, others = partners(count)
    barrier = pltpu.get_barrier_semaphore()
    for _, other in others:
        pl.semaphore_signal(barrier, inc=1, device_id={"wall": other}, device_id_type=MESH)
    buf[0] = q_edges[...]
    pl.semaphore_wait(barrier, len(others))
    exchange(count, nf, table, buf, got, send, recv, xl, xr)
    out[0] = xl[...]
    out[1] = xr[...]


def dot3(ah, al, bh, bl):
    one = functools.partial(jnp.dot, preferred_element_type=jnp.float32)
    return one(ah, bh) + (one(al, bh) + one(ah, bl))


def halves(x):
    hi = x.astype(jnp.bfloat16)
    return hi, (x - hi.astype(jnp.float32)).astype(jnp.bfloat16)


def main_kernel(f_ref, u_ref, v_ref, bc_ref, prev_ref, next_ref, m_ref, g_ref, t_ref, a_ref, q_ref,
                pad, rows, fh, fl):
    height, width = f_ref.shape[1], f_ref.shape[2]
    strip = prev_ref.shape[3]
    extra = rows.shape[0]
    mh, ml = halves(m_ref[...])
    gh, gl = halves(g_ref[0])
    pad[:, :strip] = prev_ref[0, 0]
    pad[:, strip + width :] = next_ref[0, 0]
    pad[:, strip : strip + width] = f_ref[0]
    total = width + 2 * strip
    for r in range(0, height, 16):
        x = pad[r : r + 16, :]

        def at(offset):
            return pltpu.roll(x, (total - offset) % total, 1)

        sw = (45.0 * (at(1) - at(-1)) - 9.0 * (at(2) - at(-2)) + (at(3) - at(-3))) * (1.0 / 60.0)
        t_ref[0, r : r + 16, :] = u_ref[0, r : r + 16, :] * sw[:, strip : strip + width]
    rows[...] = jnp.zeros(rows.shape, jnp.float32)
    for i in range(6):
        for t in range(width // lane):
            rows[i : i + 1, t * lane : (t + 1) * lane] = bc_ref[i, 0, t : t + 1, :]
    step = 256
    for c in range(0, width, step):
        cs = slice(c, c + step)
        fh[:height], fl[:height] = halves(f_ref[0, :, cs])
        fh[height:], fl[height:] = halves(rows[:, cs])
        slope = dot3(mh, ml, fh[...], fl[...])
        t = -(t_ref[0, :, cs] + v_ref[0, :, cs] * slope)
        t_ref[0, :, cs] = t
        f = f_ref[0, :, cs]
        rh, rl = halves(2.0 * f + time_step * t)
        q = dot3(gh, gl, rh, rl)
        a_ref[0, :, cs] = q - f
        for t in range(step // lane):
            ts = slice(t * lane, (t + 1) * lane)
            q_ref[0, 0, c // lane + t : c // lane + t + 1, :] = q[:1, ts]
            q_ref[1, 0, c // lane + t : c // lane + t + 1, :] = q[height - 1 :, ts]


def last_kernel(a_ref, x_ref, w_ref, o_ref):
    width = a_ref.shape[2]
    for t in range(width // lane):
        ts = slice(t * lane, (t + 1) * lane)
        o_ref[0, :, ts] = (a_ref[0, :, ts] + w_ref[0, 0] * x_ref[0, 0, t : t + 1, :]
                           + w_ref[0, 1] * x_ref[1, 0, t : t + 1, :])


def on_device(count, streams, fields, wall_velocity, diffusion):
    nf, nz, height, width = fields.shape
    planes = nf * nz
    tiles = width // lane
    f32 = jnp.float32
    steps = int(math.log2(count))
    flat = fields.reshape(planes, height, width)
    me = lax.axis_index("wall")

    operator = compact_operator(height)
    extra = 16
    wide = np.zeros((height, height + extra), np.float32)
    wide[:, : height + 6] = operator
    gamma1 = float(operator[0, height + 4])
    eta1 = float(operator[0, height + 5])
    ends = [[float(operator[j, height + i]) for i in range(4)] for j in (0, height - 1)]
    coef = np.stack([np.repeat(operator[j, :height, None], lane, 1) for j in (0, height - 1)]).astype(np.float32)

    larger = 0.5 * (1.0 + 2.0 * diffusion + jnp.sqrt(1.0 + 4.0 * diffusion))
    base = diffusion / larger
    log = jnp.log(base)[:, None, None]

    def rising(k):
        return 1.0 - jnp.exp(2.0 * k.astype(f32) * log)

    def green(i, j):
        most, least = jnp.maximum(i, j), jnp.minimum(i, j)
        scale = (larger * (1.0 - base * base))[:, None, None] * rising(jnp.full((1, 1), height + 1))
        return jnp.exp((most - least).astype(f32) * log) * rising(least + 1) * rising(height - most) / scale

    ids = jnp.arange(height, dtype=jnp.int32)
    inverse = green(ids[:, None], ids[None, :])
    rate = diffusion[:, None, None]
    weights = rate[:, None] * jnp.stack(
        [green(ids[:, None], jnp.full((1, lane), e)) for e in (0, height - 1)], axis=1)
    corner = diffusion[:, None] * green(jnp.zeros((1, 2), jnp.int32), jnp.array([[0, height - 1]]))[:, 0]
    table1 = merge_table(jnp.full((nf,), gamma1, f32), jnp.full((nf,), eta1, f32), count, me)
    table2 = merge_table(corner[:, 0], corner[:, 1], count, me)

    vmem = pl.BlockSpec(memory_space=pltpu.VMEM)
    smem = pl.BlockSpec(memory_space=pltpu.SMEM)
    hbm = pl.BlockSpec(memory_space=pl.ANY)
    nrecv = 1 if streams == 2 else 2
    line = (planes, tiles, lane)
    dma = pltpu.SemaphoreType.DMA
    bc, strips = pl.pallas_call(
        functools.partial(first_kernel, count, streams, nf, ends),
        out_shape=(
            jax.ShapeDtypeStruct((6,) + line, f32),
            jax.ShapeDtypeStruct((nrecv, planes, height, lane), f32),
        ),
        in_specs=[smem, vmem, hbm],
        out_specs=(vmem, vmem),
        scratch_shapes=[
            pltpu.VMEM((planes, height, width), f32),
            pltpu.VMEM((2, planes, sub, width), f32),
            pltpu.VMEM((4, 2) + line, f32),
            pltpu.VMEM((planes, height, lane), f32),
            pltpu.VMEM((nrecv, planes, height, lane), f32),
            pltpu.VMEM((steps, 2) + line, f32),
            pltpu.VMEM((steps, 2) + line, f32),
            pltpu.VMEM(line, f32),
            pltpu.VMEM(line, f32),
            dma((planes + 2,)), dma((2,)), dma((2,)), dma((nrecv,)), dma((nrecv,)),
            dma((steps,)), dma((steps,)),
        ],
        compiler_params=pltpu.CompilerParams(
            collective_id=0, has_side_effects=True, vmem_limit_bytes=40 * 2**20),
    )(table1, jnp.asarray(coef), flat)

    plane = lambda k, z: k * nz + z
    block = (1, height, width)
    tend, part, q_edges = pl.pallas_call(
        main_kernel,
        grid=(nz, nf),
        out_shape=(
            jax.ShapeDtypeStruct(flat.shape, f32),
            jax.ShapeDtypeStruct(flat.shape, f32),
            jax.ShapeDtypeStruct((2,) + line, f32),
        ),
        in_specs=[
            pl.BlockSpec(block, lambda z, k: (plane(k, z), 0, 0)),
            pl.BlockSpec(block, lambda z, k: (z, 0, 0)),
            pl.BlockSpec(block, lambda z, k: (z, 0, 0)),
            pl.BlockSpec((6, 1, tiles, lane), lambda z, k: (0, plane(k, z), 0, 0)),
            pl.BlockSpec((1, 1, height, lane), lambda z, k: (0, plane(k, z), 0, 0)),
            pl.BlockSpec((1, 1, height, lane), lambda z, k: (nrecv - 1, plane(k, z), 0, 0)),
            pl.BlockSpec((height, height + extra), lambda z, k: (0, 0)),
            pl.BlockSpec((1, height, height), lambda z, k: (k, 0, 0)),
        ],
        out_specs=(
            pl.BlockSpec(block, lambda z, k: (plane(k, z), 0, 0)),
            pl.BlockSpec(block, lambda z, k: (plane(k, z), 0, 0)),
            pl.BlockSpec((2, 1, tiles, lane), lambda z, k: (0, plane(k, z), 0, 0)),
        ),
        scratch_shapes=[
            pltpu.VMEM((height, width + 2 * lane), f32),
            pltpu.VMEM((extra, width), f32),
            pltpu.VMEM((height + extra, 256), jnp.bfloat16),
            pltpu.VMEM((height + extra, 256), jnp.bfloat16),
        ],
        compiler_params=pltpu.CompilerParams(vmem_limit_bytes=40 * 2**20),
    )(flat, flat, wall_velocity, bc, strips, strips, jnp.asarray(wide), inverse)

    beyond = pl.pallas_call(
        functools.partial(second_kernel, count, nf),
        out_shape=jax.ShapeDtypeStruct((2,) + line, f32),
        in_specs=[smem, vmem],
        out_specs=vmem,
        scratch_shapes=[
            pltpu.VMEM((steps, 2) + line, f32),
            pltpu.VMEM((steps, 2) + line, f32),
            pltpu.VMEM(line, f32),
            pltpu.VMEM(line, f32),
            dma((steps,)), dma((steps,)),
        ],
        compiler_params=pltpu.CompilerParams(collective_id=1, has_side_effects=True),
    )(table2, q_edges)

    advanced = pl.pallas_call(
        last_kernel,
        grid=(planes,),
        out_shape=jax.ShapeDtypeStruct(flat.shape, f32),
        in_specs=[
            pl.BlockSpec(block, lambda p: (p, 0, 0)),
            pl.BlockSpec((2, 1, tiles, lane), lambda p: (0, p, 0, 0)),
            pl.BlockSpec((1, 2, height, lane), lambda p: (p // nz, 0, 0, 0)),
        ],
        out_specs=pl.BlockSpec(block, lambda p: (p, 0, 0)),
        input_output_aliases={0: 0},
        compiler_params=pltpu.CompilerParams(vmem_limit_bytes=40 * 2**20),
    )(part, beyond, weights)
    return tend.reshape(fields.shape), advanced.reshape(fields.shape)


def solution(mesh):
    in_specs = (P(None, None, "wall", "stream"), P(None, "wall", "stream"), P())
    out_specs = (P(None, None, "wall", "stream"), P(None, None, "wall", "stream"))
    body = functools.partial(on_device, mesh.shape["wall"], mesh.shape["stream"])
    return jax.shard_map(body, mesh=mesh, in_specs=in_specs, out_specs=out_specs, check_vma=False)
```

time: 341 us -> 85.8 us (0.25); the launches traced: 336 us -> 85.3 us
  blocking collectives: 164 us -> 0 us
  matrix products: 96.8 us -> 0 us
  Pallas kernels: 0 us -> 73.1 us
  local copies, waits for them, and re-layouts: 42.1 us -> 6.71 us
  other arithmetic: 21.9 us -> 4.37 us
  starting transfers between devices: 7.95 us -> 0 us
    all_gather x4 -> x0, blocking collectives: 164 us -> none  [the longest x2 85 us: line_solve(): lax.all_gather(local[None, :, :, -1, :], 'wall', axis=0, tiled=True)]
    dot_general x6 -> x0, matrix products: 96.8 us -> none  [the longest x2 57.2 us: line_solve(): settled = jnp.einsum('fjl,fzlx->fzjx', backward, primed, precision=highest)]
    pallas_call x0 -> x4, Pallas kernels: none -> 73.1 us  [the longest x1 26.8 us: on_device(): pl.pallas_call(functools.partial(first_kernel, count, streams, nf, ends),...]
    slice x36 -> x0, local copies, waits for them, and re-layouts: 25.4 us -> none  [the longest x30 21.6 us: edge_tables(): return (entry[:, -1], leave_first, through)]
    ppermute x4 -> x0, starting transfers between devices: 7.95 us -> none  [the longest x1 6.13 us: with_halo(): lax.ppermute(tail, axis, [(i, (i + 1) % count) for i in range(ends)])]
    unnamed x167 -> x14, local copies, waits for them, and re-layouts: 12.4 us -> 5.69 us
    reduce_sum x7 -> x0, other arithmetic: 6.6 us -> none  [edge_tables(): through = jnp.sum(first_row * entry, axis=1)]
    select_n x5 -> x4, other arithmetic: 4.83 us -> 0.06 us  [the longest x3 0.04 us: merge_table(): add_r = jnp.where(right, rl, rr)]
  transfers between devices with their start and end apart: 4 -> 0, of which waited for: 0 -> 0; matrix products, arithmetic and copies ran while one was open for 17% -> 0% of each run, Pallas kernels for 0% -> 0%
where the time goes in v1:
time: 85.8 us; the launch traced here: 85.3 us
  Pallas kernels  73.1 us (85%)
  local copies, waits for them, and re-layouts  6.71 us (8%)
  other arithmetic  4.37 us (5%)
  between operations  1.12 us (1%)
    pallas_call x1, Pallas kernels, on_device(): pl.pallas_call(functools.partial(first_kernel, count, streams, nf, ends),...  26.8 us
    pallas_call x1, Pallas kernels, on_device(): pl.pallas_call(main_kernel, grid=(nz, nf), out_shape=(jax.ShapeDtypeStruc...  19.3 us
    pallas_call x1, Pallas kernels, on_device(): pl.pallas_call(functools.partial(second_kernel, count, nf), out_shape=jax...  17.1 us
    pallas_call x1, Pallas kernels, on_device(): pl.pallas_call(last_kernel, grid=(planes,), out_shape=jax.ShapeDtypeStruc...  9.95 us
    unnamed x14, local copies, waits for them, and re-layouts  5.69 us

profile of v1, /device:TPU:0, one launch (start us, length us, event | category | flops | bytes accessed | tf_op | source)
XLA Modules:
  0.0 85.3 jit_solution(11103043240934863883)
XLA Ops:
  0.6 0.0 copy-start.4
  0.6 0.0 copy-start.2
  1.0 0.9 %exponential_subtract_fusion = (f32[5]{0:T(128)S(1)}, f32[5]{0:T(128)S(1)}) fusion(f32[5]{0:T(128)} %param.8), kind=kLoop, calls=%fused_computation.52 | loop fusion | flops 45 | bytes 60 | tf_op jit(solution)/shard_map/sub | solution.py:309
  1.9 0.7 fusion.21
  2.6 0.8 divide_multiply_fusion
  3.5 0.1 reshape.762.table
  3.8 0.7 reshape.764.table
  4.5 0.1 convert_multiply_fusion
  4.6 0.5 multiply_divide_fusion.g_ref
  5.1 0.5 multiply_divide_fusion.2
  5.7 0.8 maximum_multiply_fusion.w_ref
  6.5 0.0 copy-start
  6.5 3.2 %copy-done = f32[5,2,192,1024]{3,2,1,0:T(8,128)S(1)} copy-done((f32[5,2,192,1024]{3,2,1,0:T(8,128)S(1)}, f32[5,2,192,1024]{3,2,1,0:T(8,128)}, u32[]{:S(2)}) %copy-start) | copy-done | bytes 7864344
  9.7 0.0 copy-start.5
  9.7 0.9 %copy-done.5 = f32[2,192,128]{2,1,0:T(8,128)S(1)} copy-done((f32[2,192,128]{2,1,0:T(8,128)S(1)}, f32[2,192,128]{2,1,0:T(8,128)}, u32[]{:S(2)}) %copy-start.5) | copy-done | bytes 196632
  10.6 0.0 copy-start.1
  10.6 26.8 %shard_map.77 = (f32[6,10,8,128]{3,2,1,0:T(8,128)S(1)}, f32[1,10,192,128]{3,2,1,0:T(8,128)S(1)}) custom-call(f32[100]{0:T(128)S(1)} %reshape.762.table, f32[2,192,128]{2,1,0:T(8,128)S(1)} %copy-done.5, f32[10,192,1024]{2,1,0:T(8,128)S(1)} %bitcast.45), custom_call_target="tpu_custom_call" | custom-call | tf_op jit(solution)/shard_map/pallas_call | solution.py:331
  37.4 0.0 copy-done.4
  37.4 0.0 copy-done.2
  37.4 0.0 copy-done.1
  37.4 19.3 %shard_map.78 = (f32[10,192,1024]{2,1,0:T(8,128)}, f32[10,192,1024]{2,1,0:T(8,128)}, f32[2,10,8,128]{3,2,1,0:T(8,128)S(1)}) custom-call(f32[10,192,1024]{2,1,0:T(8,128)S(1)} %bitcast.46, f32[10,192,1024]{2,1,0:T(8,128)S(1)} %bitcast.47, f32[2,192,1024]{2,1,0:T(8,128)S(1)} %copy-done.2, f32[6,10,8,128]{3,2,1,0:T(8,128)S(1)} %get-tuple-element.7.bc_ref, ...), custom_call_target="tpu_custom_call" | custom-call | tf_op jit(solution)/shard_map/pallas_call | solution.py:358
  56.7 0.0 copy-start.6
  56.7 0.6 copy-done.6
  57.3 17.1 %shard_map.79.x_ref = f32[2,10,8,128]{3,2,1,0:T(8,128)} custom-call(f32[100]{0:T(128)} %reshape.764.table, f32[2,10,8,128]{3,2,1,0:T(8,128)} %copy-done.6), custom_call_target="tpu_custom_call" | custom-call | tf_op jit(solution)/shard_map/pallas_call | solution.py:390
  74.5 0.0 copy-start.3
  74.5 0.9 %copy-done.3 = f32[2,10,8,128]{3,2,1,0:T(8,128)S(1)} copy-done((f32[2,10,8,128]{3,2,1,0:T(8,128)S(1)}, f32[2,10,8,128]{3,2,1,0:T(8,128)}, u32[]{:S(2)}) %copy-start.3) | copy-done | bytes 81944
  75.4 10.0 %shard_map.80 = f32[10,192,1024]{2,1,0:T(8,128)} custom-call(f32[10,192,1024]{2,1,0:T(8,128)} %get-tuple-element.10.a_ref, f32[2,10,8,128]{3,2,1,0:T(8,128)S(1)} %copy-done.3, f32[5,2,192,128]{3,2,1,0:T(8,128)S(1)} %maximum_multiply_fusion.w_ref), custom_call_target="tpu_custom_call", output_to_operand_aliasing={{}: (0, {})} | custom-call | tf_op jit(solution)/shard_map/pallas_call | solution.py:405
  (31 shorter events, 0.4 us)
Async XLA Ops:
  0.6 36.8 %copy-start.4 = (f32[192,208]{1,0:T(8,128)S(1)}, f32[192,208]{1,0:T(8,128)}, u32[]{:S(2)}) copy-start(f32[192,208]{1,0:T(8,128)} %constant.136.clone.m_ref) | copy-start | bytes 479236
  0.6 36.8 %copy-start.2 = (f32[2,192,1024]{2,1,0:T(8,128)S(1)}, f32[2,192,1024]{2,1,0:T(8,128)}, u32[]{:S(2)}) copy-start(f32[2,192,1024]{2,1,0:T(8,128)} %v_ref.1) | copy-start | bytes 4718596
  6.5 3.2 %copy-start = (f32[5,2,192,1024]{3,2,1,0:T(8,128)S(1)}, f32[5,2,192,1024]{3,2,1,0:T(8,128)}, u32[]{:S(2)}) copy-start(f32[5,2,192,1024]{3,2,1,0:T(8,128)} %param.6) | copy-start | bytes 23592964
  9.7 0.9 %copy-start.5 = (f32[2,192,128]{2,1,0:T(8,128)S(1)}, f32[2,192,128]{2,1,0:T(8,128)}, u32[]{:S(2)}) copy-start(f32[2,192,128]{2,1,0:T(8,128)} %constant.135.clone.coef) | copy-start | bytes 589828
  10.6 26.8 %copy-start.1 = (f32[5,2,192,1024]{3,2,1,0:T(8,128)S(1)}, f32[5,2,192,1024]{3,2,1,0:T(8,128)}, u32[]{:S(2)}) copy-start(f32[5,2,192,1024]{3,2,1,0:T(8,128)} %param.6) | copy-start | bytes 23592964
  56.7 0.6 copy-start.6
  74.5 0.9 %copy-start.3 = (f32[2,10,8,128]{3,2,1,0:T(8,128)S(1)}, f32[2,10,8,128]{3,2,1,0:T(8,128)}, u32[]{:S(2)}) copy-start(f32[2,10,8,128]{3,2,1,0:T(8,128)} %shard_map.79.x_ref) | copy-start | bytes 245764

commit v2 on v1

v2 whole, which is shorter than its diff:
```python
import functools
import math

import jax
import jax.numpy as jnp
import numpy as np
from jax import lax
from jax.experimental import pallas as pl
from jax.experimental.pallas import tpu as pltpu
from jax.sharding import PartitionSpec as P

MESH = pl.DeviceIdType.MESH
compact_alpha = 1.0 / 3.0
compact_near = 14.0 / 9.0
compact_far = 1.0 / 9.0
time_step = 0.25
lane = 128
sub = 8


def compact_operator(height):
    band = compact_alpha
    a = np.eye(height) + band * (np.eye(height, k=1) + np.eye(height, k=-1))
    wide = np.zeros((height, height + 4))
    for j in range(height):
        wide[j, j + 3] += 0.5 * compact_near
        wide[j, j + 1] -= 0.5 * compact_near
        wide[j, j + 4] += 0.25 * compact_far
        wide[j, j] -= 0.25 * compact_far
    source = np.concatenate(
        [wide[:, 2 : height + 2], wide[:, :2], wide[:, height + 2 :], np.zeros((height, 2))], axis=1
    )
    source[0, height + 4] = -band
    source[height - 1, height + 5] = -band
    return np.linalg.solve(a, source)


def merge_table(gamma, eta, steps, me):
    one, zero = jnp.ones_like(gamma), jnp.zeros_like(gamma)
    ll, lr, rl, rr = one, zero, zero, one
    rows = []
    for step in range(steps):
        right = (me // 2**step) % 2 == 1
        inv = 1.0 / (1.0 - gamma * gamma)
        near, far = inv * eta, inv * eta * gamma
        rows.append((inv, gamma, eta, jnp.where(right, ll, lr), jnp.where(right, rl, rr)))
        ll, lr = (
            jnp.where(right, ll * near, ll + lr * far),
            jnp.where(right, lr + ll * far, lr * near),
        )
        rl, rr = (
            jnp.where(right, rl * near, rl + rr * far),
            jnp.where(right, rr + rl * far, rr * near),
        )
        gamma, eta = gamma + eta * eta * gamma * inv, eta * eta * inv
    return rows


def diffusive_band(rate):
    larger = 0.5 * (1.0 + 2.0 * rate + jnp.sqrt(1.0 + 4.0 * rate))
    base = rate / larger
    return larger, base, jnp.log(base)


def rising(k, log):
    return 1.0 - jnp.exp(2.0 * k * log)


def edge_weights(rate, ids, height, end):
    larger, base, log = diffusive_band(rate)
    first = ids + 1.0 if end else height - ids
    away = (height - 1.0) - ids if end else ids
    scale = larger * (1.0 - base * base) * rising(height + 1.0, log)
    return rate * jnp.exp(away * log) * rising(first, log) * rising(1.0, log) / scale


def row_to_tile(dst, row):
    for t in range(row.shape[-1] // lane):
        dst[t : t + 1, :] = row[:, t * lane : (t + 1) * lane]


def dot3(ah, al, bh, bl):
    one = functools.partial(jnp.dot, preferred_element_type=jnp.float32)
    return one(ah, bh) + (one(al, bh) + one(ah, bl))


def halves(x):
    hi = x.astype(jnp.bfloat16)
    return hi, (x - hi.astype(jnp.float32)).astype(jnp.bfloat16)


def big_kernel(count, streams, nf, nz, ends, corners, rates, coef, operator, fields, velocity,
               tend, part, beyond,
               planes, wv, edge, halo, sides, strips, buf, got, near, table,
               mh, ml, gh, gl, rows, pad, fh, fl,
               local_sem, wv_sem, hs, hr, ss, sr, send, recv):
    me = lax.axis_index("wall")
    col = lax.axis_index("stream")
    steps = buf.shape[1]
    np_, height, width = planes.shape
    strip = sides.shape[2]
    tiles = width // lane
    tops = pltpu.make_async_copy(fields.at[:, pl.ds(0, sub)], edge.at[0], local_sem.at[np_])
    bots = pltpu.make_async_copy(fields.at[:, pl.ds(height - sub, sub)], edge.at[1], local_sem.at[np_ + 1])
    tops.start()
    bots.start()

    def load(p):
        return pltpu.make_async_copy(fields.at[p], planes.at[p], local_sem.at[p])

    for p in range(np_):
        load(p).start()
    speed = pltpu.make_async_copy(velocity, wv, wv_sem)
    speed.start()
    halo[2:4] = jnp.zeros((2,) + halo.shape[1:], jnp.float32)
    nexts = [lax.rem(col + 1, streams)]
    if streams > 2:
        nexts.append(lax.rem(col + streams - 1, streams))
    has_left, has_right = me > 0, me < count - 1
    others = [me + 2**s * (1 - 2 * ((me // 2**s) % 2)) for s in range(steps)]
    barrier = pltpu.get_barrier_semaphore()
    for other in others:
        pl.semaphore_signal(barrier, inc=1, device_id={"wall": other}, device_id_type=MESH)
    for other in nexts:
        pl.semaphore_signal(barrier, inc=1, device_id={"stream": other}, device_id_type=MESH)

    @pl.when(has_left)
    def _():
        pl.semaphore_signal(barrier, inc=1, device_id={"wall": me - 1}, device_id_type=MESH)

    @pl.when(has_right)
    def _():
        pl.semaphore_signal(barrier, inc=1, device_id={"wall": me + 1}, device_id_type=MESH)

    tops.wait()
    bots.wait()
    for p in range(np_):
        for r in range(2):
            row_to_tile(halo.at[0, r, p], edge[0, p, r : r + 1, :])
            row_to_tile(halo.at[1, r, p], edge[1, p, sub - 2 + r : sub - 1 + r, :])
    pl.semaphore_wait(
        barrier,
        len(others) + len(nexts) + has_left.astype(jnp.int32) + has_right.astype(jnp.int32),
    )
    to_left = pltpu.make_async_remote_copy(
        src_ref=halo.at[0], dst_ref=halo.at[3], send_sem=hs.at[0], recv_sem=hr.at[0],
        device_id={"wall": me - 1}, device_id_type=MESH)
    to_right = pltpu.make_async_remote_copy(
        src_ref=halo.at[1], dst_ref=halo.at[2], send_sem=hs.at[1], recv_sem=hr.at[1],
        device_id={"wall": me + 1}, device_id_type=MESH)

    @pl.when(has_left)
    def _():
        to_left.start()

    @pl.when(has_right)
    def _():
        to_right.start()

    def side(i, p):
        return pltpu.make_async_remote_copy(
            src_ref=sides.at[p], dst_ref=strips.at[i, p], send_sem=ss.at[i, p], recv_sem=sr.at[i, p],
            device_id={"stream": nexts[i]}, device_id_type=MESH)

    low = lax.broadcasted_iota(jnp.int32, (height, strip), 1) < strip // 2

    @pl.loop(0, np_)
    def _(p):
        load(p).wait()
        sides[p] = jnp.where(low, planes[p, :, :strip], planes[p, :, width - strip :])
        for i in range(len(nexts)):
            side(i, p).start()
        field, z = p // nz, p % nz
        for t in range(tiles):
            f = planes[p, :, t * lane : (t + 1) * lane]
            for e in range(2):
                buf[0, 0, field, e, z, t : t + 1, :] = jnp.sum(f * coef[e], axis=0, keepdims=True)

    @pl.when(has_left)
    def _():
        to_left.wait_send()
        to_right.wait_recv()

    @pl.when(has_right)
    def _():
        to_right.wait_send()
        to_left.wait_recv()

    for m, (gamma, eta) in enumerate(corners):
        rows_ = merge_table(jnp.full((tiles, lane), gamma), jnp.full((tiles, lane), eta), steps, me)
        for s in range(steps):
            for c in range(5):
                for k in range(nf):
                    table[m, s, c, k] = rows_[s][c]
    near[...] = jnp.zeros(near.shape, jnp.float32)
    for k in range(nf):
        for e in range(2):
            at = pl.ds(k * nz, nz)
            buf[0, 0, k, e] = (buf[0, 0, k, e]
                               + ends[e][0] * halo[2, 0, at] + ends[e][1] * halo[2, 1, at]
                               + ends[e][2] * halo[3, 0, at] + ends[e][3] * halo[3, 1, at])

    def trade(m, s, k):
        return pltpu.make_async_remote_copy(
            src_ref=buf.at[m, s, k], dst_ref=got.at[m, s, k],
            send_sem=send.at[m, s, k], recv_sem=recv.at[m, s, k],
            device_id={"wall": others[s]}, device_id_type=MESH)

    def merge(m, s, k):
        trade(m, s, k).wait()
        right = (me // 2**s) % 2 == 1
        inv, gamma, eta, add_l, add_r = (table[m, s, c, k] for c in range(5))
        fo, lo, fp, lp = buf[m, s, k, 0], buf[m, s, k, 1], got[m, s, k, 0], got[m, s, k, 1]
        f1, l1 = jnp.where(right, fp, fo), jnp.where(right, lp, lo)
        f2, l2 = jnp.where(right, fo, fp), jnp.where(right, lo, lp)
        ahead = inv * (f2 + gamma * l1)
        behind = inv * (l1 + gamma * f2)
        if s + 1 < steps:
            buf[m, s + 1, k, 0] = f1 + eta * ahead
            buf[m, s + 1, k, 1] = l2 + eta * behind
            trade(m, s + 1, k).start()
        value = jnp.where(right, behind, ahead)
        near[m, k, 0] += add_l * value
        near[m, k, 1] += add_r * value

    @pl.loop(0, nf)
    def _(k):
        trade(0, 0, k).start()

    mh[...], ml[...] = halves(operator[...])
    row = lax.broadcasted_iota(jnp.int32, (height, height), 0).astype(jnp.float32)
    column = lax.broadcasted_iota(jnp.int32, (height, height), 1).astype(jnp.float32)
    down = lax.broadcasted_iota(jnp.int32, (height, 1), 0).astype(jnp.float32)
    along = lax.broadcasted_iota(jnp.int32, (1, height), 1).astype(jnp.float32)

    @pl.loop(0, nf)
    def _(k):
        larger, base, log = diffusive_band(jnp.full((1, height), rates[k], jnp.float32))
        _, _, tall = diffusive_band(jnp.full((height, 1), rates[k], jnp.float32))
        scale = 1.0 / (larger * (1.0 - base * base) * rising(height + 1.0, log))
        upper = rising(down + 1.0, tall) * (rising(height - along, log) * scale)
        lower = rising(height - down, tall) * (rising(along + 1.0, log) * scale)
        green = jnp.exp(jnp.abs(row - column) * log) * jnp.where(row <= column, upper, lower)
        gh[k], gl[k] = halves(green)
        rate = jnp.full((tiles, lane), rates[k], jnp.float32)
        gamma = edge_weights(rate, jnp.zeros((tiles, lane), jnp.float32), height, 0)
        eta = edge_weights(rate, jnp.zeros((tiles, lane), jnp.float32), height, 1)
        for s, cs in enumerate(merge_table(gamma, eta, steps, me)):
            for c in range(5):
                table[1, s, c, k] = cs[c]

    total = width + 2 * strip

    def sweep(p):
        for i in range(len(nexts)):
            side(i, p).wait()
        pad[:, :strip] = strips[0, p]
        pad[:, strip + width :] = strips[len(nexts) - 1, p]
        pad[:, strip : strip + width] = planes[p]
        z = p % nz

        @pl.loop(0, height, step=16)
        def _(r):
            at_rows = pl.ds(pl.multiple_of(r, 16), 16)
            x = pad[at_rows, :]

            def at(offset):
                return pltpu.roll(x, (total - offset) % total, 1)

            sw = (45.0 * (at(1) - at(-1)) - 9.0 * (at(2) - at(-2)) + (at(3) - at(-3))) * (1.0 / 60.0)
            tend[p, at_rows, :] = planes[z, at_rows, :] * sw[:, strip : strip + width]

    for s in range(steps):
        pl.loop(s * np_ // steps, (s + 1) * np_ // steps)(sweep)
        pl.loop(0, nf)(functools.partial(merge, 0, s))
    speed.wait()
    step = 256
    rows[...] = jnp.zeros(rows.shape, jnp.float32)

    def plane(k, z):
        p = k * nz + z
        for t in range(tiles):
            ts = slice(t * lane, (t + 1) * lane)
            for r in range(2):
                rows[r : r + 1, ts] = halo[2, r, p, t : t + 1, :]
                rows[2 + r : 3 + r, ts] = halo[3, r, p, t : t + 1, :]
                rows[4 + r : 5 + r, ts] = near[0, k, r, z, t : t + 1, :]
        for c in range(0, width, step):
            cs = slice(c, c + step)
            f = planes[p, :, cs]
            fh[:height, cs], fl[:height, cs] = halves(f)
            fh[height:, cs], fl[height:, cs] = halves(rows[:, cs])
            slope = dot3(mh[...], ml[...], fh[:, cs], fl[:, cs])
            t_ = -(tend[p, :, cs] + wv[z, :, cs] * slope)
            tend[p, :, cs] = t_
            rh, rl = halves(2.0 * f + time_step * t_)
            q = dot3(gh[k], gl[k], rh, rl)
            part[p, :, cs] = q - f
            for t in range(step // lane):
                ts = slice(t * lane, (t + 1) * lane)
                at_t = slice(c // lane + t, c // lane + t + 1)
                buf[1, 0, k, 0, z, at_t, :] = q[:1, ts]
                buf[1, 0, k, 1, z, at_t, :] = q[height - 1 :, ts]

    @pl.loop(0, nf + steps)
    def _(k):
        @pl.when(k < nf)
        def _():
            pl.loop(0, nz)(functools.partial(plane, k))
            trade(1, 0, k).start()

        for s in range(steps):
            @pl.when(jnp.logical_and(k >= s + 1, k < nf + s + 1))
            def _():
                merge(1, s, k - 1 - s)

    beyond[...] = near[1]


def last_kernel(rates, tend, part, near, t_out, a_out, stage, sem):
    np_, height, width = part.shape
    nf = near.shape[0]
    nz = np_ // nf
    first = pltpu.make_async_copy(tend, t_out, sem.at[np_])
    first.start()
    ids = lax.broadcasted_iota(jnp.int32, (height, lane), 0).astype(jnp.float32)

    def put(p):
        return pltpu.make_async_copy(stage.at[p], a_out.at[p], sem.at[p])

    @pl.loop(0, nf)
    def _(k):
        rate = jnp.full((height, lane), rates[k], jnp.float32)
        wl, wr = (edge_weights(rate, ids, height, e) for e in range(2))
        for z in range(nz):
            p = k * nz + z
            for t in range(width // lane):
                ts = slice(t * lane, (t + 1) * lane)
                stage[p, :, ts] = (part[p, :, ts] + wl * near[k, 0, z, t : t + 1, :]
                                   + wr * near[k, 1, z, t : t + 1, :])
            put(p).start()

    @pl.loop(0, np_)
    def _(p):
        put(p).wait()

    first.wait()


def on_device(count, streams, fields, wall_velocity, diffusion):
    nf, nz, height, width = fields.shape
    planes = nf * nz
    tiles = width // lane
    f32 = jnp.float32
    bf16 = jnp.bfloat16
    steps = int(math.log2(count))
    flat = fields.reshape(planes, height, width)
    operator = compact_operator(height)
    extra = 16
    wide = np.zeros((height, height + extra), np.float32)
    wide[:, : height + 6] = operator
    corners = [(float(operator[0, height + 4]), float(operator[0, height + 5]))]
    ends = [[float(operator[j, height + i]) for i in range(4)] for j in (0, height - 1)]
    coef = np.stack([np.repeat(operator[j, :height, None], lane, 1) for j in (0, height - 1)]).astype(np.float32)

    vmem = pl.BlockSpec(memory_space=pltpu.VMEM)
    smem = pl.BlockSpec(memory_space=pltpu.SMEM)
    hbm = pl.BlockSpec(memory_space=pltpu.HBM)
    nrecv = 1 if streams == 2 else 2
    tile = (tiles, lane)
    dma = pltpu.SemaphoreType.DMA
    whole = jax.ShapeDtypeStruct(flat.shape, f32)
    tend, part, beyond = pl.pallas_call(
        functools.partial(big_kernel, count, streams, nf, nz, ends, corners),
        out_shape=(whole, whole, jax.ShapeDtypeStruct((nf, 2, nz) + tile, f32)),
        in_specs=[smem, vmem, vmem, hbm, hbm],
        out_specs=(vmem, vmem, vmem),
        scratch_shapes=[
            pltpu.VMEM((planes, height, width), f32),
            pltpu.VMEM((nz, height, width), f32),
            pltpu.VMEM((2, planes, sub, width), f32),
            pltpu.VMEM((4, 2, planes) + tile, f32),
            pltpu.VMEM((planes, height, lane), f32),
            pltpu.VMEM((nrecv, planes, height, lane), f32),
            pltpu.VMEM((2, steps, nf, 2, nz) + tile, f32),
            pltpu.VMEM((2, steps, nf, 2, nz) + tile, f32),
            pltpu.VMEM((2, nf, 2, nz) + tile, f32),
            pltpu.VMEM((2, steps, 5, nf) + tile, f32),
            pltpu.VMEM((height, height + extra), bf16),
            pltpu.VMEM((height, height + extra), bf16),
            pltpu.VMEM((nf, height, height), bf16),
            pltpu.VMEM((nf, height, height), bf16),
            pltpu.VMEM((extra, width), f32),
            pltpu.VMEM((height, width + 2 * lane), f32),
            pltpu.VMEM((height + extra, width), bf16),
            pltpu.VMEM((height + extra, width), bf16),
            dma((planes + 2,)), dma, dma((2,)), dma((2,)),
            dma((nrecv, planes)), dma((nrecv, planes)),
            dma((2, steps, nf)), dma((2, steps, nf)),
        ],
        compiler_params=pltpu.CompilerParams(
            collective_id=0, has_side_effects=True, vmem_limit_bytes=36 * 2**20),
    )(diffusion, jnp.asarray(coef), jnp.asarray(wide), flat, wall_velocity)

    tendency, advanced = pl.pallas_call(
        last_kernel,
        out_shape=(whole, whole),
        in_specs=[smem, vmem, vmem, vmem],
        out_specs=(hbm, hbm),
        scratch_shapes=[pltpu.VMEM(flat.shape, f32), dma((planes + 1,))],
        compiler_params=pltpu.CompilerParams(vmem_limit_bytes=16 * 2**20),
    )(diffusion, tend, part, beyond)
    return tendency.reshape(fields.shape), advanced.reshape(fields.shape)


def solution(mesh):
    in_specs = (P(None, None, "wall", "stream"), P(None, "wall", "stream"), P())
    out_specs = (P(None, None, "wall", "stream"), P(None, None, "wall", "stream"))
    body = functools.partial(on_device, mesh.shape["wall"], mesh.shape["stream"])
    return jax.shard_map(body, mesh=mesh, in_specs=in_specs, out_specs=out_specs, check_vma=False)
```

time: 85.8 us -> 73.3 us (0.85)
  Pallas kernels: 73.1 us -> 68.5 us
  other arithmetic: 4.37 us -> 0 us
  local copies, waits for them, and re-layouts: 6.71 us -> 3.91 us
    pallas_call x4 -> x2, Pallas kernels: 73.1 us -> 68.5 us  [the longest x1 62.3 us: on_device(): pl.pallas_call(functools.partial(big_kernel, count, streams, nf, nz, ends...]
    unnamed x14 -> x8, local copies, waits for them, and re-layouts: 5.69 us -> 3.91 us
    mul x5 -> x0, other arithmetic: 1.63 us -> none  [the longest x1 0.8 us: on_device(): rate[:, None]]
    div x3 -> x0, other arithmetic: 1.06 us -> none  [the longest x2 1.05 us: green(): jnp.exp((most - least).astype(f32) * log) * rising(least + 1)]
    sub x1 -> x0, other arithmetic: 0.88 us -> none  [rising(): return 1.0 - jnp.exp(2.0 * k.astype(f32) * log)]
where the time goes in v2:
time: 73.3 us; the launch traced here: 73.1 us
  Pallas kernels  68.5 us (93%)
  local copies, waits for them, and re-layouts  3.91 us (5%)
    pallas_call x1, Pallas kernels, on_device(): pl.pallas_call(functools.partial(big_kernel, count, streams, nf, nz, ends...  62.3 us
    pallas_call x1, Pallas kernels, on_device(): pl.pallas_call(last_kernel, out_shape=(whole, whole), in_specs=[smem, vme...  6.23 us
    unnamed x8, local copies, waits for them, and re-layouts  3.91 us

profile of v2, /device:TPU:0, one launch (start us, length us, event | category | flops | bytes accessed | tf_op | source)
XLA Modules:
  0.0 73.1 jit_solution(7655477333776458816)
XLA Ops:
  0.6 0.0 copy-start
  0.6 1.4 %copy-done = f32[2,192,1024]{2,1,0:T(8,128)S(1)} copy-done((f32[2,192,1024]{2,1,0:T(8,128)S(1)}, f32[2,192,1024]{2,1,0:T(8,128)}, u32[]{:S(2)}) %copy-start) | copy-done | bytes 1572888
  2.0 0.0 copy-start.1
  2.0 0.9 %copy-done.1 = f32[192,208]{1,0:T(8,128)S(1)} copy-done((f32[192,208]{1,0:T(8,128)S(1)}, f32[192,208]{1,0:T(8,128)}, u32[]{:S(2)}) %copy-start.1) | copy-done | bytes 159768
  3.0 0.0 copy-start.2
  3.0 0.9 %copy-done.2 = f32[2,192,128]{2,1,0:T(8,128)S(1)} copy-done((f32[2,192,128]{2,1,0:T(8,128)S(1)}, f32[2,192,128]{2,1,0:T(8,128)}, u32[]{:S(2)}) %copy-start.2) | copy-done | bytes 196632
  3.9 0.0 copy-start.3
  3.9 0.7 copy-done.3
  4.5 62.3 %shard_map.68 = (f32[10,192,1024]{2,1,0:T(8,128)S(1)}, f32[10,192,1024]{2,1,0:T(8,128)S(1)}, f32[5,2,2,8,128]{4,3,2,1,0:T(8,128)S(1)}) custom-call(f32[5]{0:T(128)S(1)} %copy-done.3, f32[2,192,128]{2,1,0:T(8,128)S(1)} %copy-done.2, f32[192,208]{1,0:T(8,128)S(1)} %copy-done.1, f32[10,192,1024]{2,1,0:T(8,128)} %bitcast.3, f32[2,192,1024]{2,1,0:T(8,128)S(1)} %copy-done), custom_call_target="tpu_custom_call" | custom-call | tf_op jit(solution)/shard_map/pallas_call | solution.py:373
  66.9 6.2 %shard_map.69 = (f32[10,192,1024]{2,1,0:T(8,128)}, f32[10,192,1024]{2,1,0:T(8,128)}) custom-call(f32[5]{0:T(128)S(1)} %copy-done.3, f32[10,192,1024]{2,1,0:T(8,128)S(1)} %get-tuple-element.7.tend, f32[10,192,1024]{2,1,0:T(8,128)S(1)} %get-tuple-element.8.part, f32[5,2,2,8,128]{4,3,2,1,0:T(8,128)S(1)} %get-tuple-element.9.near), custom_call_target="tpu_custom_call" | custom-call | tf_op jit(solution)/shard_map/pallas_call | solution.py:405
Async XLA Ops:
  0.6 1.4 %copy-start = (f32[2,192,1024]{2,1,0:T(8,128)S(1)}, f32[2,192,1024]{2,1,0:T(8,128)}, u32[]{:S(2)}) copy-start(f32[2,192,1024]{2,1,0:T(8,128)} %velocity.1) | copy-start | bytes 4718596
  2.0 0.9 %copy-start.1 = (f32[192,208]{1,0:T(8,128)S(1)}, f32[192,208]{1,0:T(8,128)}, u32[]{:S(2)}) copy-start(f32[192,208]{1,0:T(8,128)} %constant.5.clone.operator) | copy-start | bytes 479236
  3.0 0.9 %copy-start.2 = (f32[2,192,128]{2,1,0:T(8,128)S(1)}, f32[2,192,128]{2,1,0:T(8,128)}, u32[]{:S(2)}) copy-start(f32[2,192,128]{2,1,0:T(8,128)} %constant.4.clone.coef) | copy-start | bytes 589828
  3.9 0.7 copy-start.3

commit v3 on v2

--- a/solution.py
+++ b/solution.py
@@ -89,11 +89,11 @@
     return hi, (x - hi.astype(jnp.float32)).astype(jnp.bfloat16)
 
 
-def big_kernel(count, streams, nf, nz, ends, corners, rates, coef, operator, fields, velocity,
+def big_kernel(count, streams, nf, nz, ends, corners, rates, coef_in, operator_in, fields, velocity,
                tend, part, beyond,
-               planes, wv, edge, halo, sides, strips, buf, got, near, table,
-               mh, ml, gh, gl, rows, pad, fh, fl,
-               local_sem, wv_sem, hs, hr, ss, sr, send, recv):
+               coef, operator, planes, wv, edge, halo, sides, strips, buf, got, near, table,
+               mh, ml, gh, gl, rows, ph, pq, stencil, fh, fl,
+               const_sem, local_sem, wv_sem, hs, hr, ss, sr, send, recv):
     me = lax.axis_index("wall")
     col = lax.axis_index("stream")
     steps = buf.shape[1]
@@ -104,6 +104,12 @@
     bots = pltpu.make_async_copy(fields.at[:, pl.ds(height - sub, sub)], edge.at[1], local_sem.at[np_ + 1])
     tops.start()
     bots.start()
+    consts = [
+        pltpu.make_async_copy(coef_in, coef, const_sem.at[0]),
+        pltpu.make_async_copy(operator_in, operator, const_sem.at[1]),
+    ]
+    for const in consts:
+        const.start()
 
     def load(p):
         return pltpu.make_async_copy(fields.at[p], planes.at[p], local_sem.at[p])
@@ -162,6 +168,8 @@
             src_ref=sides.at[p], dst_ref=strips.at[i, p], send_sem=ss.at[i, p], recv_sem=sr.at[i, p],
             device_id={"stream": nexts[i]}, device_id_type=MESH)
 
+    for const in consts:
+        const.wait()
     low = lax.broadcasted_iota(jnp.int32, (height, strip), 1) < strip // 2
 
     @pl.loop(0, np_)
@@ -249,32 +257,32 @@
             for c in range(5):
                 table[1, s, c, k] = cs[c]
 
-    total = width + 2 * strip
+    step = 256
+    gap = (lax.broadcasted_iota(jnp.int32, (step + 2 * strip, step), 0)
+           - lax.broadcasted_iota(jnp.int32, (step + 2 * strip, step), 1) - strip)
+    size = jnp.abs(gap)
+    taps = jnp.where(size == 1, 45.0, jnp.where(size == 2, -9.0, jnp.where(size == 3, 1.0, 0.0)))
+    stencil[...] = jnp.where(gap < 0, -taps, taps).astype(jnp.bfloat16)
 
     def sweep(p):
         for i in range(len(nexts)):
             side(i, p).wait()
-        pad[:, :strip] = strips[0, p]
-        pad[:, strip + width :] = strips[len(nexts) - 1, p]
-        pad[:, strip : strip + width] = planes[p]
+        ph[:, :strip], pq[:, :strip] = halves(strips[0, p])
+        ph[:, strip + width :], pq[:, strip + width :] = halves(strips[len(nexts) - 1, p])
         z = p % nz
-
-        @pl.loop(0, height, step=16)
-        def _(r):
-            at_rows = pl.ds(pl.multiple_of(r, 16), 16)
-            x = pad[at_rows, :]
-
-            def at(offset):
-                return pltpu.roll(x, (total - offset) % total, 1)
-
-            sw = (45.0 * (at(1) - at(-1)) - 9.0 * (at(2) - at(-2)) + (at(3) - at(-3))) * (1.0 / 60.0)
-            tend[p, at_rows, :] = planes[z, at_rows, :] * sw[:, strip : strip + width]
+        for c in range(0, width, step):
+            cs = slice(strip + c, strip + c + step)
+            ph[:, cs], pq[:, cs] = halves(planes[p, :, c : c + step])
+        for c in range(0, width, step):
+            cs = slice(c, c + step + 2 * strip)
+            sw = (jnp.dot(ph[:, cs], stencil[...], preferred_element_type=jnp.float32)
+                  + jnp.dot(pq[:, cs], stencil[...], preferred_element_type=jnp.float32)) * (1.0 / 60.0)
+            tend[p, :, c : c + step] = planes[z, :, c : c + step] * sw
 
     for s in range(steps):
         pl.loop(s * np_ // steps, (s + 1) * np_ // steps)(sweep)
         pl.loop(0, nf)(functools.partial(merge, 0, s))
     speed.wait()
-    step = 256
     rows[...] = jnp.zeros(rows.shape, jnp.float32)
 
     def plane(k, z):
@@ -302,18 +310,13 @@
                 buf[1, 0, k, 0, z, at_t, :] = q[:1, ts]
                 buf[1, 0, k, 1, z, at_t, :] = q[height - 1 :, ts]
 
-    @pl.loop(0, nf + steps)
+    @pl.loop(0, nf)
     def _(k):
-        @pl.when(k < nf)
-        def _():
-            pl.loop(0, nz)(functools.partial(plane, k))
-            trade(1, 0, k).start()
-
-        for s in range(steps):
-            @pl.when(jnp.logical_and(k >= s + 1, k < nf + s + 1))
-            def _():
-                merge(1, s, k - 1 - s)
-
+        pl.loop(0, nz)(functools.partial(plane, k))
+        trade(1, 0, k).start()
+
+    for s in range(steps):
+        pl.loop(0, nf)(functools.partial(merge, 1, s))
     beyond[...] = near[1]
 
 
@@ -373,9 +376,11 @@
     tend, part, beyond = pl.pallas_call(
         functools.partial(big_kernel, count, streams, nf, nz, ends, corners),
         out_shape=(whole, whole, jax.ShapeDtypeStruct((nf, 2, nz) + tile, f32)),
-        in_specs=[smem, vmem, vmem, hbm, hbm],
+        in_specs=[smem, hbm, hbm, hbm, hbm],
         out_specs=(vmem, vmem, vmem),
         scratch_shapes=[
+            pltpu.VMEM(coef.shape, f32),
+            pltpu.VMEM(wide.shape, f32),
             pltpu.VMEM((planes, height, width), f32),
             pltpu.VMEM((nz, height, width), f32),
             pltpu.VMEM((2, planes, sub, width), f32),
@@ -391,10 +396,12 @@
             pltpu.VMEM((nf, height, height), bf16),
             pltpu.VMEM((nf, height, height), bf16),
             pltpu.VMEM((extra, width), f32),
-            pltpu.VMEM((height, width + 2 * lane), f32),
+            pltpu.VMEM((height, width + 2 * lane), bf16),
+            pltpu.VMEM((height, width + 2 * lane), bf16),
+            pltpu.VMEM((256 + 2 * lane, 256), bf16),
             pltpu.VMEM((height + extra, width), bf16),
             pltpu.VMEM((height + extra, width), bf16),
-            dma((planes + 2,)), dma, dma((2,)), dma((2,)),
+            dma((2,)), dma((planes + 2,)), dma, dma((2,)), dma((2,)),
             dma((nrecv, planes)), dma((nrecv, planes)),
             dma((2, steps, nf)), dma((2, steps, nf)),
         ],

time: 73.3 us -> 61.3 us (0.84)
  Pallas kernels: 68.5 us -> 56.6 us
    pallas_call x1, Pallas kernels: 62.3 us -> 50.3 us  [on_device(): pl.pallas_call(functools.partial(big_kernel, count, streams, nf, nz, ends...]
where the time goes in v3:
time: 61.3 us; the launch traced here: 61.1 us
  Pallas kernels  56.6 us (92%)
  local copies, waits for them, and re-layouts  3.91 us (6%)
  between operations  0.65 us (1%)
    pallas_call x1, Pallas kernels, on_device(): pl.pallas_call(functools.partial(big_kernel, count, streams, nf, nz, ends...  50.3 us
    pallas_call x1, Pallas kernels, on_device(): pl.pallas_call(last_kernel, out_shape=(whole, whole), in_specs=[smem, vme...  6.23 us
    unnamed x8, local copies, waits for them, and re-layouts  3.91 us

profile of v3, /device:TPU:0, one launch (start us, length us, event | category | flops | bytes accessed | tf_op | source)
XLA Modules:
  0.0 61.1 jit_solution(18174136764125430248)
XLA Ops:
  0.6 0.0 copy-start
  0.6 1.4 %copy-done = f32[2,192,1024]{2,1,0:T(8,128)S(1)} copy-done((f32[2,192,1024]{2,1,0:T(8,128)S(1)}, f32[2,192,1024]{2,1,0:T(8,128)}, u32[]{:S(2)}) %copy-start) | copy-done | bytes 1572888
  2.0 0.0 copy-start.1
  2.0 0.9 %copy-done.1 = f32[192,208]{1,0:T(8,128)S(1)} copy-done((f32[192,208]{1,0:T(8,128)S(1)}, f32[192,208]{1,0:T(8,128)}, u32[]{:S(2)}) %copy-start.1) | copy-done | bytes 159768
  3.0 0.0 copy-start.2
  3.0 0.9 %copy-done.2 = f32[2,192,128]{2,1,0:T(8,128)S(1)} copy-done((f32[2,192,128]{2,1,0:T(8,128)S(1)}, f32[2,192,128]{2,1,0:T(8,128)}, u32[]{:S(2)}) %copy-start.2) | copy-done | bytes 196632
  3.9 0.0 copy-start.3
  3.9 0.7 %copy-done.3 = f32[5]{0:T(128)S(1)} copy-done((f32[5]{0:T(128)S(1)}, f32[5]{0:T(128)}, u32[]{:S(2)}) %copy-start.3) | copy-done | bytes 44
  4.5 50.3 %shard_map.68 = (f32[10,192,1024]{2,1,0:T(8,128)S(1)}, f32[10,192,1024]{2,1,0:T(8,128)S(1)}, f32[5,2,2,8,128]{4,3,2,1,0:T(8,128)S(1)}) custom-call(f32[5]{0:T(128)S(1)} %copy-done.3, f32[2,192,128]{2,1,0:T(8,128)S(1)} %copy-done.2, f32[192,208]{1,0:T(8,128)S(1)} %copy-done.1, f32[10,192,1024]{2,1,0:T(8,128)} %bitcast.3, f32[2,192,1024]{2,1,0:T(8,128)S(1)} %copy-done), custom_call_target="tpu_custom_call" | custom-call | tf_op jit(solution)/shard_map/pallas_call | solution.py:376
  54.9 6.2 %shard_map.69 = (f32[10,192,1024]{2,1,0:T(8,128)}, f32[10,192,1024]{2,1,0:T(8,128)}) custom-call(f32[5]{0:T(128)S(1)} %copy-done.3, f32[10,192,1024]{2,1,0:T(8,128)S(1)} %get-tuple-element.7.tend, f32[10,192,1024]{2,1,0:T(8,128)S(1)} %get-tuple-element.8.part, f32[5,2,2,8,128]{4,3,2,1,0:T(8,128)S(1)} %get-tuple-element.9.near), custom_call_target="tpu_custom_call" | custom-call | tf_op jit(solution)/shard_map/pallas_call | solution.py:412
Async XLA Ops:
  0.6 1.4 %copy-start = (f32[2,192,1024]{2,1,0:T(8,128)S(1)}, f32[2,192,1024]{2,1,0:T(8,128)}, u32[]{:S(2)}) copy-start(f32[2,192,1024]{2,1,0:T(8,128)} %velocity.1) | copy-start | bytes 4718596
  2.0 0.9 %copy-start.1 = (f32[192,208]{1,0:T(8,128)S(1)}, f32[192,208]{1,0:T(8,128)}, u32[]{:S(2)}) copy-start(f32[192,208]{1,0:T(8,128)} %constant.5.clone.operator_in) | copy-start | bytes 479236
  3.0 0.9 %copy-start.2 = (f32[2,192,128]{2,1,0:T(8,128)S(1)}, f32[2,192,128]{2,1,0:T(8,128)}, u32[]{:S(2)}) copy-start(f32[2,192,128]{2,1,0:T(8,128)} %constant.4.clone.coef_in) | copy-start | bytes 589828
  3.9 0.7 %copy-start.3 = (f32[5]{0:T(128)S(1)}, f32[5]{0:T(128)}, u32[]{:S(2)}) copy-start(f32[5]{0:T(128)} %rates.3) | copy-start | bytes 64
